TPU v7x, 256 devices: a whole 4x4x8 slice. The times are simulated.
256 devices in a mesh: orow: 16 (over z_lo, x), ocol: 16 (over z_hi, y, core).
Axes of the slice: x: 4, y: 4, z: 8 (z_hi: 2, z_lo: 4; z = z_hi * 4 + z_lo), core: 2. Of those that a mesh axis runs over, the one named last changes fastest.
Arguments:
- amplitudes: bfloat16 [16, 16, 512, 512], P('orow', 'ocol'), may hold values from -6 to 6
- tile_mask: int32 [16, 16, 2, 2], P('orow', 'ocol'), may hold values 0 or 1
- domain_tiles: int32 [16, 16, 2], replicated, may hold values from 0 to 7, as said below
- cholesky: bfloat16 [16, 2048, 2048], P('ocol'), as said below
Outputs:
- ladder_sym: float32 [16, 16, 512, 512], P('orow', 'ocol')
Inputs may be any that keep to these rules, and one draw needn't show every extreme that they name: `domain_tiles`: for every pair the 2 tile numbers differ, and pair (j, i) lists the same tiles in the same order as pair (i, j). Every vector cholesky[q] is a symmetric 2048 x 2048 matrix.
All inputs are finite; a program needn't handle non-finite values. No bound on the sum of `tile_mask` on one device may be relied on, other than what follows from the above.
Results may differ from a plain program's by a relative error of at most 0.0029.
Values may be sent and summed in bfloat16 or wider, within the bound.
A program may use at most 128 MiB of HBM per device.

v0:
```python
import jax
import jax.numpy as jnp
from jax import lax
from jax.sharding import PartitionSpec as P

TILE = 256
K = 2


def pick_tiles(local_factor, chosen):
    number = local_factor.shape[0]
    tiles = local_factor.shape[1] // TILE
    blocked = local_factor.reshape(number, tiles, TILE, tiles, TILE)
    picked = blocked[:, chosen[..., :, None], :, chosen[..., None, :], :]
    leading = chosen.ndim - 1
    permuted = tuple(range(leading)) + (leading + 2, leading, leading + 3, leading + 1, leading + 4)
    width = chosen.shape[-1] * TILE
    return picked.transpose(permuted).reshape(chosen.shape[:-1] + (number, width, width))


def masked(amplitudes, tile_mask):
    row_pairs = amplitudes.shape[0]
    col_pairs = amplitudes.shape[1]
    shaped = amplitudes.reshape(row_pairs, col_pairs, K, TILE, K, TILE)
    weights = tile_mask.astype(jnp.bfloat16)[:, :, :, None, :, None]
    return (shaped * weights).reshape(amplitudes.shape)


def shards(amplitudes, tile_mask, domain_tiles, cholesky):
    row_pairs = amplitudes.shape[0]
    row_domains = lax.dynamic_slice_in_dim(
        domain_tiles, lax.axis_index("orow") * row_pairs, row_pairs, 0
    )
    weighted = masked(amplitudes, tile_mask)
    gathered = lax.all_gather(weighted, "ocol", axis=1, tiled=True)
    factor = pick_tiles(cholesky, row_domains)
    inner = jnp.einsum(
        "ijqac,ijcd->ijqad", factor, gathered, preferred_element_type=jnp.float32
    ).astype(jnp.bfloat16)
    summed = lax.psum_scatter(
        jnp.einsum("ijqad,ijqbd->jiab", inner, factor, preferred_element_type=jnp.float32),
        "ocol",
        scatter_dimension=0,
        tiled=True,
    )
    ladder = summed.transpose(1, 0, 2, 3)
    turned = lax.all_to_all(ladder, "ocol", split_axis=2, concat_axis=1, tiled=True)
    turned = lax.all_to_all(
        lax.all_to_all(turned, "orow", split_axis=1, concat_axis=0, tiled=True),
        "ocol",
        split_axis=0,
        concat_axis=2,
        tiled=True,
    )
    return ladder + turned.transpose(1, 0, 3, 2)


def solution(mesh):
    return jax.shard_map(
        shards,
        mesh=mesh,
        in_specs=(
            P("orow", "ocol", None, None),
            P("orow", "ocol", None, None),
            P(),
            P("ocol", None, None),
        ),
        out_specs=P("orow", "ocol", None, None),
        check_vma=False,
    )
```

profile of v0, /device:TPU:32, one launch (start us, length us, event | category | flops | bytes accessed | tf_op | source)
XLA Modules:
  0.0 467.5 jit_solution(741445048212051335)
XLA Ops:
  6.5 0.0 all-gather.2.cloned.1.call-start
  6.5 0.7 convert_bitcast_fusion
  7.2 0.3 mul.16
  7.6 0.3 mul.17
  7.9 1.9 bitcast_multiply_fusion
  9.8 0.0 all-gather.2.cloned.1.call-update
  9.8 0.0 reduce-scatter.2.cloned.1.call-start
  9.9 0.7 compare_select_fusion
  10.6 0.1 copy.29
  10.7 0.1 reshape.87
  10.8 10.3 %copy.40 = bf16[256,8,8,256]{3,2,1,0:T(8,128)(2,1)} copy(bf16[256,8,8,256]{3,1,2,0:T(8,128)(2,1)} %bitcast.45) | data formatting | bytes 16777216
  21.1 8.8 %copy.30 = bf16[8,256,8,256]{3,1,2,0:T(8,128)(2,1)} copy(bf16[8,256,8,256]{3,2,1,0:T(8,128)(2,1)} %bitcast.44) | data formatting | bytes 16777216 | tf_op jit(solution)/shard_map/reshape | solution.py:13
  29.9 9.4 %gather_fusion = bf16[64,256,256]{2,1,0:T(8,128)(2,1)} fusion(bf16[8,256,8,256]{3,1,2,0:T(8,128)(2,1)} %copy.30, s32[64]{0:T(128)S(1)} %reshape.87), kind=kCustom, calls=%fused_computation | custom fusion | bytes 16777728 | tf_op jit(solution)/shard_map/gather | solution.py:14
  39.4 16.3 %copy.31 = bf16[1,16,1,2,256,2,256]{6,5,4,3,1,2,0:T(2,128)(2,1)} copy(bf16[1,16,1,2,256,2,256]{6,4,5,3,1,2,0:T(8,128)(2,1)} %bitcast.43) | data formatting | bytes 16777216 | tf_op jit(solution)/shard_map/transpose | solution.py:18
  55.6 14.2 %reshape.81 = bf16[16,512,512]{2,1,0:T(8,128)(2,1)} reshape(bf16[1,16,1,2,256,2,256]{6,5,4,3,1,2,0:T(2,128)(2,1)} %copy.31) | data formatting | bytes 16777216 | tf_op jit(solution)/shard_map/reshape.10
  69.9 50.2 %all-gather.2.cloned.1.call-done = bf16[1,16,512,512]{3,2,0,1:T(8,128)(2,1)} async-done(((bf16[1,1,512,512]{3,2,0,1:T(8,128)(2,1)}), bf16[1,16,512,512]{3,2,0,1:T(8,128)(2,1)}) %all-gather.2.cloned.1.call-update) | async-done | bytes 8388624 | tf_op jit(solution)/shard_map/all_gather | solution.py:35
  120.1 22.0 %convolution_bitcast_fusion = f32[16,1,512,512]{3,2,0,1:T(8,128)} fusion(bf16[16,512,512]{2,1,0:T(8,128)(2,1)} %reshape.81, bf16[1,16,512,512]{3,2,0,1:T(8,128)(2,1)} %all-gather.2.cloned.1.call-done), kind=kOutput, calls=%fused_computation.1 | convolution fusion | flops 8594128896 | bytes 33554432 | tf_op jit(solution)/shard_map/ijqad,ijqbd->jiab/dot_general | solution.py:41
  142.0 0.0 reduce-scatter.2.cloned.1.call-update
  142.0 213.5 %reduce-scatter.2.cloned.1.call-done = f32[1,1,512,512]{3,2,0,1:T(8,128)} async-done(((f32[16,1,512,512]{3,2,0,1:T(8,128)}), f32[1,1,512,512]{3,2,0,1:T(8,128)}) %reduce-scatter.2.cloned.1.call-update) | async-done | bytes 1048592 | tf_op jit(solution)/shard_map/reduce_scatter | solution.py:40
  355.5 0.0 copy-start
  355.5 2.4 copy.33
  357.9 34.7 %all_to_all.36 = f32[1,1,512,512]{3,0,1,2:T(1,128)S(1)} all-to-all(f32[1,1,512,512]{3,0,1,2:T(1,128)S(1)} %copy.33), channel_id=1, replica_groups=mesh['orow'=16,'ocol'=16] {'ocol'}, dimensions={2} | all-to-all | bytes 2097152 | tf_op jit(solution)/shard_map/all_to_all | solution.py:47
  392.6 0.1 copy.34
  392.7 32.2 %all_to_all.37 = f32[1,16,32,512]{3,2,0,1:T(8,128)S(1)} all-to-all(f32[1,16,32,512]{3,2,0,1:T(8,128)S(1)} %copy.34), channel_id=1, replica_groups=mesh['orow'=16,'ocol'=16] {'orow'}, dimensions={1} | all-to-all | bytes 2097152 | tf_op jit(solution)/shard_map/all_to_all | solution.py:49
  424.9 34.2 %all_to_all.38 = f32[16,1,32,512]{3,2,1,0:T(8,128)S(1)} all-to-all(f32[16,1,32,512]{3,2,1,0:T(8,128)S(1)} %bitcast.47), channel_id=1, replica_groups=mesh['orow'=16,'ocol'=16] {'ocol'}, dimensions={0} | all-to-all | bytes 2097152 | tf_op jit(solution)/shard_map/all_to_all | solution.py:48
  459.1 0.3 copy.36
  459.5 0.0 copy-done
  459.5 1.2 fusion.7
  (5 shorter events, 0.0 us)
Async XLA Ops:
  6.5 113.5 %all-gather.2.cloned.1.call-start = ((), (), s32[]{:S(2)}) async-start(), calls=%async_computation.4 | async-start | bytes 8912896 | tf_op jit(solution)/shard_map/all_gather | solution.py:35
  9.8 345.7 %reduce-scatter.2.cloned.1.call-start = ((), (), s32[]{:S(2)}) async-start(), calls=%async_computation.5 | async-start | bytes 17825792 | tf_op jit(solution)/shard_map/reduce_scatter | solution.py:40
  355.5 103.9 %copy-start = (f32[1,1,512,512]{3,2,0,1:T(8,128)S(1)}, f32[1,1,512,512]{3,2,0,1:T(8,128)}, u32[]{:S(2)}) copy-start(f32[1,1,512,512]{3,2,0,1:T(8,128)} %reduce-scatter.2.cloned.1.call-done) | copy-start | bytes 3145732
Sparse Core Ops, SparseCore 0:
  10.1 109.9 all-gather.1
  142.2 213.3 reduce-scatter.1
where the time goes:
time: 468 us; the launch traced here: 467 us
  waiting for transfers between devices  264 us (56%)
  blocking collectives  101 us (22%)
  local copies, waits for them, and re-layouts  62.7 us (13%)
  matrix products  22 us (5%)
  between operations  13.5 us (3%)
    reduce_scatter x1, waiting for transfers between devices, shards(): lax.psum_scatter(jnp.einsum('ijqad,ijqbd->jiab', inner, factor, preferred...  213 us
    all_gather x1, waiting for transfers between devices, shards(): gathered = lax.all_gather(weighted, 'ocol', axis=1, tiled=True)  50.2 us
    all_to_all x1, blocking collectives, shards(): lax.all_to_all(ladder, 'ocol', split_axis=2, concat_axis=1, tiled=True)  34.7 us
    all_to_all x1, blocking collectives, shards(): lax.all_to_all(lax.all_to_all(turned, 'orow', split_axis=1, concat_axis=0...  34.2 us
    all_to_all x1, blocking collectives, shards(): lax.all_to_all(turned, 'orow', split_axis=1, concat_axis=0, tiled=True)  32.2 us
    dot_general x1, matrix products, shards(): jnp.einsum('ijqad,ijqbd->jiab', inner, factor, preferred_element_type=jnp...  22 us
    transpose x1, local copies, waits for them, and re-layouts, pick_tiles(): picked.transpose(permuted)  16.3 us
    another operation x1, local copies, waits for them, and re-layouts  14.2 us
  transfers between devices with their start and end apart: 2, of which 2 were waited for; matrix products, arithmetic and copies ran while one was open for 13% of the time, Pallas kernels for 0%

commit v1 on v0

--- a/solution.py
+++ b/solution.py
@@ -45,13 +45,11 @@
     )
     ladder = summed.transpose(1, 0, 2, 3)
     turned = lax.all_to_all(ladder, "ocol", split_axis=2, concat_axis=1, tiled=True)
-    turned = lax.all_to_all(
-        lax.all_to_all(turned, "orow", split_axis=1, concat_axis=0, tiled=True),
-        "ocol",
-        split_axis=0,
-        concat_axis=2,
-        tiled=True,
-    )
+    x = lax.all_to_all(turned, "orow", split_axis=1, concat_axis=0, tiled=True)
+    count = lax.axis_size("ocol")
+    blocks = jnp.stack(jnp.split(x, count, axis=0), axis=0)
+    blocks = lax.all_to_all(blocks, "ocol", split_axis=0, concat_axis=0)
+    turned = jnp.concatenate(blocks, axis=2)
     return ladder + turned.transpose(1, 0, 3, 2)
 
 

time: 468 us -> 468 us (level)
    unnamed x3 -> x18, local copies, waits for them, and re-layouts: 10.3 us -> 10.4 us
    another operation x1 -> x2, local copies, waits for them, and re-layouts: 14.2 us -> 14.2 us
where the time goes in v1:
time: 468 us
  waiting for transfers between devices  264 us (56%)
  blocking collectives  101 us (22%)
  local copies, waits for them, and re-layouts  62.9 us (13%)
  matrix products  22 us (5%)
  between operations  13.6 us (3%)
    reduce_scatter x1, waiting for transfers between devices, shards(): lax.psum_scatter(jnp.einsum('ijqad,ijqbd->jiab', inner, factor, preferred...  213 us
    all_gather x1, waiting for transfers between devices, shards(): gathered = lax.all_gather(weighted, 'ocol', axis=1, tiled=True)  50.2 us
    all_to_all x1, blocking collectives, shards(): lax.all_to_all(ladder, 'ocol', split_axis=2, concat_axis=1, tiled=True)  34.7 us
    all_to_all x1, blocking collectives, shards(): blocks = lax.all_to_all(blocks, 'ocol', split_axis=0, concat_axis=0)  34.2 us
    all_to_all x1, blocking collectives, shards(): x = lax.all_to_all(turned, 'orow', split_axis=1, concat_axis=0, tiled=True)  32.2 us
    dot_general x1, matrix products, shards(): jnp.einsum('ijqad,ijqbd->jiab', inner, factor, preferred_element_type=jnp...  22 us
    transpose x1, local copies, waits for them, and re-layouts, pick_tiles(): picked.transpose(permuted)  16.3 us
    another operation x1, local copies, waits for them, and re-layouts  14.2 us
  transfers between devices with their start and end apart: 2, of which 2 were waited for; matrix products, arithmetic and copies ran while one was open for 13% of the time, Pallas kernels for 0%

profile of v1, /device:TPU:32, one launch (start us, length us, event | category | flops | bytes accessed | tf_op | source)
XLA Modules:
  0.0 467.7 jit_solution(5482543911931519086)
XLA Ops:
  6.5 0.0 all-gather.2.cloned.1.call-start
  6.5 0.7 convert_bitcast_fusion
  7.2 0.3 mul.16
  7.6 0.3 mul.17
  7.9 1.9 bitcast_multiply_fusion
  9.8 0.0 all-gather.2.cloned.1.call-update
  9.8 0.0 reduce-scatter.2.cloned.1.call-start
  9.9 0.7 compare_select_fusion
  10.6 0.1 copy.87
  10.7 0.1 reshape.120
  10.8 10.3 %copy.111 = bf16[256,8,8,256]{3,2,1,0:T(8,128)(2,1)} copy(bf16[256,8,8,256]{3,1,2,0:T(8,128)(2,1)} %bitcast.117) | data formatting | bytes 16777216
  21.1 8.8 %copy.88 = bf16[8,256,8,256]{3,1,2,0:T(8,128)(2,1)} copy(bf16[8,256,8,256]{3,2,1,0:T(8,128)(2,1)} %bitcast.116) | data formatting | bytes 16777216 | tf_op jit(solution)/shard_map/reshape | solution.py:13
  29.9 9.4 %gather_fusion = bf16[64,256,256]{2,1,0:T(8,128)(2,1)} fusion(bf16[8,256,8,256]{3,1,2,0:T(8,128)(2,1)} %copy.88, s32[64]{0:T(128)S(1)} %reshape.120), kind=kCustom, calls=%fused_computation | custom fusion | bytes 16777728 | tf_op jit(solution)/shard_map/gather | solution.py:14
  39.4 16.3 %copy.89 = bf16[1,16,1,2,256,2,256]{6,5,4,3,1,2,0:T(2,128)(2,1)} copy(bf16[1,16,1,2,256,2,256]{6,4,5,3,1,2,0:T(8,128)(2,1)} %bitcast.115) | data formatting | bytes 16777216 | tf_op jit(solution)/shard_map/transpose | solution.py:18
  55.6 14.2 %reshape.113 = bf16[16,512,512]{2,1,0:T(8,128)(2,1)} reshape(bf16[1,16,1,2,256,2,256]{6,5,4,3,1,2,0:T(2,128)(2,1)} %copy.89) | data formatting | bytes 16777216 | tf_op jit(solution)/shard_map/reshape.11
  69.9 50.2 %all-gather.2.cloned.1.call-done = bf16[1,16,512,512]{3,2,0,1:T(8,128)(2,1)} async-done(((bf16[1,1,512,512]{3,2,0,1:T(8,128)(2,1)}), bf16[1,16,512,512]{3,2,0,1:T(8,128)(2,1)}) %all-gather.2.cloned.1.call-update) | async-done | bytes 8388624 | tf_op jit(solution)/shard_map/all_gather | solution.py:35
  120.1 22.0 %convolution_bitcast_fusion = f32[16,1,512,512]{3,2,0,1:T(8,128)} fusion(bf16[16,512,512]{2,1,0:T(8,128)(2,1)} %reshape.113, bf16[1,16,512,512]{3,2,0,1:T(8,128)(2,1)} %all-gather.2.cloned.1.call-done), kind=kOutput, calls=%fused_computation.1 | convolution fusion | flops 8594128896 | bytes 33554432 | tf_op jit(solution)/shard_map/ijqad,ijqbd->jiab/dot_general | solution.py:41
  142.0 0.0 reduce-scatter.2.cloned.1.call-update
  142.0 213.5 %reduce-scatter.2.cloned.1.call-done = f32[1,1,512,512]{3,2,0,1:T(8,128)} async-done(((f32[16,1,512,512]{3,2,0,1:T(8,128)}), f32[1,1,512,512]{3,2,0,1:T(8,128)}) %reduce-scatter.2.cloned.1.call-update) | async-done | bytes 1048592 | tf_op jit(solution)/shard_map/reduce_scatter | solution.py:40
  355.5 0.0 copy-start
  355.5 2.4 copy.91
  357.9 34.7 %all_to_all.29 = f32[1,1,512,512]{3,0,1,2:T(1,128)S(1)} all-to-all(f32[1,1,512,512]{3,0,1,2:T(1,128)S(1)} %copy.91), channel_id=1, replica_groups=mesh['orow'=16,'ocol'=16] {'ocol'}, dimensions={2} | all-to-all | bytes 2097152 | tf_op jit(solution)/shard_map/all_to_all | solution.py:47
  392.6 0.1 copy.92
  392.7 32.2 %all_to_all.30 = f32[1,16,32,512]{3,2,0,1:T(8,128)S(1)} all-to-all(f32[1,16,32,512]{3,2,0,1:T(8,128)S(1)} %copy.92), channel_id=1, replica_groups=mesh['orow'=16,'ocol'=16] {'orow'}, dimensions={1} | all-to-all | bytes 2097152 | tf_op jit(solution)/shard_map/all_to_all | solution.py:48
  425.1 34.2 %all_to_all.31 = f32[16,1,1,32,512]{4,3,2,1,0:T(8,128)S(1)} all-to-all(f32[16,1,1,32,512]{4,3,2,1,0:T(8,128)S(1)} %fusion.8), channel_id=1, replica_groups=mesh['orow'=16,'ocol'=16] {'ocol'}, dimensions={0} | all-to-all | bytes 2097152 | tf_op jit(solution)/shard_map/all_to_all | solution.py:51
  459.4 0.3 copy.107
  459.7 0.0 copy-done
  459.7 1.2 fusion.7
  (21 shorter events, 0.1 us)
Async XLA Ops:
  6.5 113.5 %all-gather.2.cloned.1.call-start = ((), (), s32[]{:S(2)}) async-start(), calls=%async_computation.4 | async-start | bytes 8912896 | tf_op jit(solution)/shard_map/all_gather | solution.py:35
  9.8 345.7 %reduce-scatter.2.cloned.1.call-start = ((), (), s32[]{:S(2)}) async-start(), calls=%async_computation.5 | async-start | bytes 17825792 | tf_op jit(solution)/shard_map/reduce_scatter | solution.py:40
  355.5 104.2 %copy-start = (f32[1,1,512,512]{3,2,0,1:T(8,128)S(1)}, f32[1,1,512,512]{3,2,0,1:T(8,128)}, u32[]{:S(2)}) copy-start(f32[1,1,512,512]{3,2,0,1:T(8,128)} %reduce-scatter.2.cloned.1.call-done) | copy-start | bytes 3145732
Sparse Core Ops, SparseCore 0:
  10.1 109.9 all-gather.1
  142.2 213.3 reduce-scatter.1
